TPU v7x, 32 devices: a whole 2x2x4 slice. The times are simulated.
32 devices in a mesh: row: 8 (over y, x, core), rep: 4 (over z).
Axes of the slice: x: 2, y: 2, z: 4, core: 2. Of those that a mesh axis runs over, the one named last changes fastest.
Arguments:
- features: bfloat16 [8192, 256], P('row'), may hold values from -6 to 6
- weight_self: bfloat16 [256, 256], replicated, may hold values from -0.375 to 0.375
- weight_neigh: bfloat16 [256, 256], replicated, may hold values from -0.375 to 0.375
- degrees: int32 [8192], P('row'), may hold values from 1 to 47
- tile_values: bfloat16 [8, 8, 48, 128, 128], P('row', 'rep'), may hold values from 0 to 1
- tile_blocks: int32 [8, 8, 48, 2], P('row', 'rep'), may hold values from 0 to 7
- tile_count: int32 [8, 8], P('row', 'rep'), may hold values from 1 to 48, as said below
- cotangent: bfloat16 [8192, 256], P(('row', 'rep')), may hold values from -6 to 6
Outputs:
- output: bfloat16 [8192, 256], P(('row', 'rep'))
- grad_self: float32 [256, 256], replicated
- grad_neigh: float32 [256, 256], replicated
- grad_features: bfloat16 [8192, 256], P(('row', 'rep'))
Inputs may be any that keep to these rules, and one draw needn't show every extreme that they name: `tile_count`: for some row index and section all 48 slots are live in every draw.
All inputs are finite; a program needn't handle non-finite values.
Results may differ from a plain program's by a relative error of at most 0.024.
Values may be sent and summed in bfloat16 or wider, within the bound.
A program may use at most 64 MiB of HBM per device.

v0:
```python
import jax
import jax.numpy as jnp
from jax import lax
from jax.sharding import PartitionSpec as P


def from_root(value, axis, source):
    kept = jnp.where(lax.axis_index(axis) == source, value, 0).astype(value.dtype)
    return lax.psum(kept, axis)


def hot_tables(blocks, count, nblk, slots):
    live = (jnp.arange(slots) < count).astype(jnp.float32)
    dest_hot = (blocks[:, 0][:, None] == jnp.arange(nblk)[None, :]).astype(jnp.float32) * live[
        :, None
    ]
    src_hot = (blocks[:, 1][:, None] == jnp.arange(nblk)[None, :]).astype(jnp.float32)
    return (dest_hot, src_hot)


def body(
    features, weight_self, weight_neigh, degrees, tile_values, tile_blocks, tile_count, cotangent
):
    rows, width = features.shape
    tile = tile_values.shape[3]
    slots = tile_values.shape[2]
    sections_here = tile_values.shape[1]
    nblk = rows // tile
    nrep = lax.axis_size("rep")
    share = rows // nrep
    rep_pos = lax.axis_index("rep")
    row_pos = lax.axis_index("row")
    partial_value = jnp.zeros((nblk, tile, width), jnp.float32)
    for section in range(sections_here):
        source = from_root(features, "row", rep_pos * sections_here + section)
        source_blocks = source.reshape(nblk, tile, width)
        dest_hot, src_hot = hot_tables(tile_blocks[0, section], tile_count[0, section], nblk, slots)
        picked = jnp.einsum(
            "tc,cif->tif",
            src_hot.astype(jnp.bfloat16),
            source_blocks,
            preferred_element_type=jnp.bfloat16,
        )
        prod = jnp.einsum(
            "tij,tjf->tif", tile_values[0, section], picked, preferred_element_type=jnp.float32
        )
        partial_value = partial_value + jnp.einsum("tb,tif->bif", dest_hot, prod)
    partial_value = partial_value.reshape(rows, width)
    degree_all = degrees.astype(jnp.float32)[:, None]
    degree_mine = lax.dynamic_slice_in_dim(degree_all, rep_pos * share, share, 0)
    feat_mine = lax.dynamic_slice_in_dim(features, rep_pos * share, share, 0)
    agg_part = lax.psum_scatter(partial_value, "rep", scatter_dimension=0, tiled=True)
    agg_mine = (agg_part / degree_mine).astype(jnp.bfloat16)
    pre = jnp.dot(feat_mine, weight_self, preferred_element_type=jnp.float32) + jnp.dot(
        agg_mine, weight_neigh, preferred_element_type=jnp.float32
    )
    sig = jax.nn.sigmoid(pre)
    gpre_mine = (cotangent.astype(jnp.float32) * sig * (1.0 + pre * (1.0 - sig))).astype(
        jnp.bfloat16
    )
    dagg_mine = (
        jnp.dot(gpre_mine, weight_neigh.T, preferred_element_type=jnp.float32) / degree_mine
    ).astype(jnp.bfloat16)
    dagg_all = lax.all_gather(dagg_mine, "rep", axis=0, tiled=True)
    output = jax.nn.silu(pre).astype(jnp.bfloat16)
    grad_self_part = jnp.dot(feat_mine.T, gpre_mine, preferred_element_type=jnp.float32)
    grad_neigh_part = jnp.dot(agg_mine.T, gpre_mine, preferred_element_type=jnp.float32)
    grad_self, grad_neigh = lax.psum((grad_self_part, grad_neigh_part), ("row", "rep"))
    dagg_blocks = dagg_all.reshape(nblk, tile, width)
    terms = []
    for section in range(sections_here):
        dest_hot, src_hot = hot_tables(tile_blocks[0, section], tile_count[0, section], nblk, slots)
        picked = jnp.einsum(
            "tb,bif->tif",
            dest_hot.astype(jnp.bfloat16),
            dagg_blocks,
            preferred_element_type=jnp.bfloat16,
        )
        contrib = jnp.einsum(
            "tij,tif->tjf", tile_values[0, section], picked, preferred_element_type=jnp.float32
        )
        terms.append(jnp.einsum("tc,tjf->cjf", src_hot, contrib).reshape(rows, width))
    stacked = jnp.stack(terms, 0)
    summed = lax.psum(stacked, "row")
    owned = lax.dynamic_index_in_dim(summed, row_pos % sections_here, 0, keepdims=False).astype(
        jnp.bfloat16
    )
    everyone = from_root(owned, "rep", row_pos // sections_here)
    back_mine = lax.dynamic_slice_in_dim(everyone, rep_pos * share, share, 0)
    grad_features = (
        jnp.dot(gpre_mine, weight_self.T, preferred_element_type=jnp.float32)
        + back_mine.astype(jnp.float32)
    ).astype(jnp.bfloat16)
    return (output, grad_self, grad_neigh, grad_features)


def solution(mesh):
    in_specs = (
        P("row", None),
        P(),
        P(),
        P("row"),
        P("row", "rep", None, None, None),
        P("row", "rep", None, None),
        P("row", "rep"),
        P(("row", "rep"), None),
    )
    out_specs = (P(("row", "rep"), None), P(), P(), P(("row", "rep"), None))
    return jax.shard_map(body, mesh=mesh, in_specs=in_specs, out_specs=out_specs, check_vma=False)
```

profile of v0, /device:TPU:7, one launch (start us, length us, event | category | flops | bytes accessed | tf_op | source)
XLA Modules:
  0.0 396.2 jit_solution(14081113110862203722)
XLA Ops:
  7.2 2.3 broadcast_select_fusion.1
  9.5 0.0 reduce-scatter.2.cloned.1.call-start
  9.6 1.3 fusion.78
  10.9 0.6 compare_convert_fusion
  11.6 0.7 compare_convert_fusion.1
  12.2 0.7 slice_bitcast_fusion.1
  13.0 53.9 %all-reduce.11.cloned.1.call-done = (bf16[8,128,256]{2,1,0:T(8,128)(2,1)}, bf16[8,128,256]{2,1,0:T(8,128)(2,1)}) async-done(((bf16[8,128,256]{2,1,0:T(8,128)(2,1)}, bf16[8,128,256]{2,1,0:T(8,128)(2,1)}), (bf16[8,128,256]{2,1,0:T(8,128)(2,1)}, bf16[8,128,256]{2,1,0:T(8,128)(2,1)})) %all-reduce.11.cloned.1.call-update) | async-done | bytes 1048592 | tf_op jit(solution)/shard_map/psum | solution.py:9
  66.9 2.1 fusion.31
  68.9 3.2 fusion.12
  72.2 3.8 copy.22
  76.0 2.2 fusion.33
  78.3 3.2 fusion.14
  81.5 4.9 %copy.19 = bf16[48,256,128]{1,0,2:T(8,128)(2,1)} copy(bf16[48,256,128]{2,1,0:T(8,128)(2,1)} %fusion.14) | data formatting | bytes 6291456 | tf_op jit(solution)/shard_map/tij,tjf->tif/dot_general | solution.py:44
  86.4 0.5 fusion.4
  86.9 1.4 copy-done.1
  88.3 0.5 fusion.24
  88.8 1.3 copy.14
  90.2 0.0 all-reduce.7.cloned.1.call-start
  90.3 0.1 dynamic-slice.3
  90.4 1.1 fusion.41
  91.4 27.3 %reduce-scatter.2.cloned.1.call-done = f32[256,256]{1,0:T(8,128)} async-done(((f32[1024,256]{1,0:T(8,128)}), f32[256,256]{1,0:T(8,128)}) %reduce-scatter.2.cloned.1.call-update) | async-done | bytes 262160 | tf_op jit(solution)/shard_map/reduce_scatter | solution.py:52
  118.8 1.9 multiply_convert_fusion
  120.7 0.2 fusion.28
  121.0 12.2 %all_gather.3 = bf16[1024,256]{1,0:T(8,128)(2,1)S(1)} all-gather(bf16[256,256]{1,0:T(8,128)(2,1)S(1)} %fusion.28), channel_id=1, replica_groups=mesh['row'=8,'rep'=4] {'rep'}, dimensions={0}, use_global_device_ids=true | all-gather | bytes 655360 | tf_op jit(solution)/shard_map/all_gather | solution.py:64
  133.1 1.0 fusion.37
  134.2 2.7 fusion.35
  136.8 3.1 fusion.10
  139.9 3.8 copy.25
  143.8 0.5 fusion.2
  144.3 1.3 copy.15
  145.6 0.2 copy-done.2
  145.8 1.2 copy-done.6
  147.0 3.1 fusion.8
  150.1 3.8 copy.27
  153.9 0.5 fusion
  154.5 0.3 copy.16
  154.8 0.4 copy-done.7
  155.2 0.1 pad_maximum_fusion
  155.3 59.9 %all-reduce.12 = bf16[2,1024,256]{2,1,0:T(8,128)(2,1)S(1)} all-reduce(f32[2,1024,256]{2,1,0:T(8,128)S(1)} %pad_maximum_fusion), channel_id=1, replica_groups=mesh['row'=8,'rep'=4] {'row'}, use_global_device_ids=true, to_apply=%region_5.6 | all-reduce | flops 524288 | bytes 3145728 | tf_op jit(solution)/shard_map/psum | solution.py:84
  215.2 0.8 fusion.30
  216.1 0.0 all-reduce.9.cloned.1.call-start
  216.1 1.8 fusion.39
  218.0 2.0 fusion.77
  220.0 32.1 %all-reduce.7.cloned.1.call-done = bf16[1024,256]{1,0:T(8,128)(2,1)} async-done(((bf16[1024,256]{1,0:T(8,128)(2,1)}), bf16[1024,256]{1,0:T(8,128)(2,1)}) %all-reduce.7.cloned.1.call-update) | async-done | bytes 524304 | tf_op jit(solution)/shard_map/psum | solution.py:9
  252.0 1.8 fusion.27
  253.8 132.5 %all-reduce.9.cloned.1.call-done = (f32[256,256]{1,0:T(8,128)}, f32[256,256]{1,0:T(8,128)}) async-done(((f32[256,256]{1,0:T(8,128)}, f32[256,256]{1,0:T(8,128)}), (f32[256,256]{1,0:T(8,128)}, f32[256,256]{1,0:T(8,128)})) %all-reduce.9.cloned.1.call-update) | async-done | bytes 524304 | tf_op jit(solution)/shard_map/psum | solution.py:68
  386.3 1.7 copy.51
  388.0 1.7 copy.52
  (37 shorter events, 0.2 us)
Async XLA Ops:
  7.2 111.6 %copy-start = (bf16[256,256]{1,0:T(8,128)(2,1)S(1)}, bf16[256,256]{1,0:T(8,128)(2,1)}, u32[]{:S(2)}) copy-start(bf16[256,256]{1,0:T(8,128)(2,1)} %param.10) | copy-start | bytes 393220
  7.2 59.7 %all-reduce.11.cloned.1.call-start = ((), (), s32[]{:S(2)}) async-start(), calls=%async_computation.4 | async-start | bytes 2097152 | tf_op jit(solution)/shard_map/psum | solution.py:9
  7.2 61.7 %copy-start.3 = (bf16[1,2,48,128,128]{4,3,2,1,0:T(8,128)(2,1)S(1)}, bf16[1,2,48,128,128]{4,3,2,1,0:T(8,128)(2,1)}, u32[]{:S(2)}) copy-start(bf16[1,2,48,128,128]{4,3,2,1,0:T(8,128)(2,1)} %param.12) | copy-start | bytes 9437188
  9.5 109.2 %reduce-scatter.2.cloned.1.call-start = ((), (), s32[]{:S(2)}) async-start(), calls=%async_computation.1 | async-start | bytes 1310720 | tf_op jit(solution)/shard_map/reduce_scatter | solution.py:52
  11.6 74.8 %copy-start.10 = (bf16[48]{0:T(256)(128)(2,1)}, bf16[48]{0:T(256)(128)(2,1)S(1)}, u32[]{:S(2)}) copy-start(bf16[48]{0:T(256)(128)(2,1)S(1)} %compare_convert_fusion) | copy-start | bytes 292
  12.2 74.7 %copy-start.12 = (bf16[48]{0:T(256)(128)(2,1)}, bf16[48]{0:T(256)(128)(2,1)S(1)}, u32[]{:S(2)}) copy-start(bf16[48]{0:T(256)(128)(2,1)S(1)} %compare_convert_fusion.1) | copy-start | bytes 292
  76.0 2.2 copy-start.4
  86.4 1.9 copy-start.1
  88.3 1.9 copy-start.9
  88.3 2.1 copy-start.8
  88.8 30.0 %copy-start.16 = (bf16[256,256]{1,0:T(8,128)(2,1)S(1)}, bf16[256,256]{1,0:T(8,128)(2,1)}, u32[]{:S(2)}) copy-start(bf16[256,256]{1,0:T(8,128)(2,1)} %param.15) | copy-start | bytes 393220
  90.1 43.0 %copy-start.13 = (bf16[48]{0:T(256)(128)(2,1)S(1)}, bf16[48]{0:T(256)(128)(2,1)}, u32[]{:S(2)}) copy-start(bf16[48]{0:T(256)(128)(2,1)} %copy-done.12) | copy-start | bytes 292
  90.2 161.9 %all-reduce.7.cloned.1.call-start = ((), (), s32[]{:S(2)}) async-start(), calls=%async_computation.2 | async-start | bytes 1048576 | tf_op jit(solution)/shard_map/psum | solution.py:9
  90.4 43.8 %copy-start.14 = (f32[256]{0:T(256)}, f32[256]{0:T(256)S(1)}, u32[]{:S(2)}) copy-start(f32[256]{0:T(256)S(1)} %dynamic-slice.3) | copy-start | bytes 3076
  120.7 13.4 %copy-start.11 = (bf16[48]{0:T(256)(128)(2,1)S(1)}, bf16[48]{0:T(256)(128)(2,1)}, u32[]{:S(2)}) copy-start(bf16[48]{0:T(256)(128)(2,1)} %copy-done.10) | copy-start | bytes 292
  133.1 3.7 copy-start.5
  143.8 2.1 copy-start.2
  143.8 3.2 copy-start.6
  153.9 1.2 copy-start.7
  155.3 62.7 %copy-start.15 = (f32[256]{0:T(256)S(1)}, f32[256]{0:T(256)}, u32[]{:S(2)}) copy-start(f32[256]{0:T(256)} %copy-done.14) | copy-start | bytes 3076
  216.1 170.2 %all-reduce.9.cloned.1.call-start = ((), (), s32[]{:S(2)}) async-start(), calls=%async_computation.3 | async-start | bytes 1048576 | tf_op jit(solution)/shard_map/psum | solution.py:68
Sparse Core Ops, SparseCore 0:
  11.2 55.6 all-reduce.10
  90.3 28.4 reduce-scatter.1
  216.2 35.8 all-reduce.6
  257.9 128.3 all-reduce.8
where the time goes:
time: 400 us; the launch traced here: 396 us
  waiting for transfers between devices  246 us (62%)
  blocking collectives  72 us (18%)
  matrix products  31.5 us (8%)
  local copies, waits for them, and re-layouts  28 us (7%)
  between operations  14 us (4%)
  other arithmetic  4.54 us (1%)
    psum x1, waiting for transfers between devices, body(): lax.psum((grad_self_part, grad_neigh_part), ('row', 'rep'))  132 us
    psum x2, waiting for transfers between devices, from_root(): return lax.psum(kept, axis)  86 us
    psum x1, blocking collectives, body(): summed = lax.psum(stacked, 'row')  59.9 us
    reduce_scatter x1, waiting for transfers between devices, body(): lax.psum_scatter(partial_value, 'rep', scatter_dimension=0, tiled=True)  27.3 us
    all_gather x1, blocking collectives, body(): dagg_all = lax.all_gather(dagg_mine, 'rep', axis=0, tiled=True)  12.2 us
    dot_general x2, local copies, waits for them, and re-layouts, body(): jnp.einsum('tij,tjf->tif', tile_values[0, section], picked, preferred_ele...  8.77 us
  transfers between devices with their start and end apart: 4, of which 4 were waited for; matrix products, arithmetic and copies ran while one was open for 3% of the time, Pallas kernels for 0%

commit v1 on v0

v1 whole, which is shorter than its diff:
```python
import functools

import jax
import jax.numpy as jnp
from jax import lax
from jax.experimental import pallas as pl
from jax.experimental.pallas import tpu as pltpu
from jax.sharding import PartitionSpec as P

MESH = pl.DeviceIdType.MESH
F32 = jnp.float32
BF16 = jnp.bfloat16
PAIR = 2


def dense_kernel(blocks_ref, count_ref, tiles_ref, out_ref, acc):
    section = pl.program_id(0)
    tile = tiles_ref.shape[-1]
    acc[...] = jnp.zeros_like(acc)

    def add(slot, carry):
        to = pl.multiple_of(blocks_ref[section, slot, 0] * tile, tile)
        src = pl.multiple_of(blocks_ref[section, slot, 1] * tile, tile)
        acc[pl.ds(to, tile), pl.ds(src, tile)] += tiles_ref[0, slot].astype(F32)
        return carry

    lax.fori_loop(0, count_ref[section], add, 0)
    out_ref[0] = acc[...].astype(BF16)


def dense_adjacency(tile_values, tile_blocks, tile_count, rows):
    sections, slots, tile, _ = tile_values.shape
    return pl.pallas_call(
        dense_kernel,
        grid=(sections,),
        out_shape=jax.ShapeDtypeStruct((sections, rows, rows), BF16),
        in_specs=[
            pl.BlockSpec(memory_space=pltpu.SMEM),
            pl.BlockSpec(memory_space=pltpu.SMEM),
            pl.BlockSpec((1, slots, tile, tile), lambda s: (s, 0, 0, 0)),
        ],
        out_specs=pl.BlockSpec((1, rows, rows), lambda s: (s, 0, 0)),
        scratch_shapes=[pltpu.VMEM((rows, rows), F32)],
        name="dense",
    )(tile_blocks, tile_count, tile_values)


def remote(src, dst, send, recv, device):
    return pltpu.make_async_remote_copy(
        src_ref=src, dst_ref=dst, send_sem=send, recv_sem=recv, device_id=device, device_id_type=MESH
    )


def layer_kernel(
    nrow, nrep, here,
    feat, wself, wneigh, deg, cot, adj_hbm,
    out, gself, gneigh, gfeat,
    adj, src, part, part_in, dagg, dagg_t, terms, pair_in, summed, plane_in, back, back_in,
    wpart, wrow_in, wrep_in, wall, base,
    adj_sem, loc_sem, a1s, a1r, a2s, a2r, a3s, a3r, bs, br, cs, cr, w1s, w1r, w2s, w2r, w3s, w3r,
    d0s, d0r, d1s, d1r, d2s, d2r,
):
    row, rep = lax.axis_index("row"), lax.axis_index("rep")
    rows, width = feat.shape
    share = rows // nrep
    half = nrow // PAIR
    hi, lo = row // PAIR, row % PAIR
    partner = (hi * PAIR + (1 - lo), rep)
    owner = (rep * here + row // nrep, row % nrep)
    giver = ((row % here) * nrep + rep, row // here)
    moves = jnp.logical_or(owner[0] != row, owner[1] != rep)

    adj_copy = pltpu.make_async_copy(adj_hbm, adj, adj_sem)
    adj_copy.start()

    barrier = pltpu.get_barrier_semaphore()

    def greet(device):
        pl.semaphore_signal(barrier, inc=1, device_id=device, device_id_type=MESH)

    for d in range(1, nrow):
        greet(((row + d) % nrow, rep))
    for d in range(1, nrep):
        greet((row, (rep + d) % nrep))

    @pl.when(moves)
    def _():
        greet(owner)
        greet(giver)

    pl.semaphore_wait(barrier, nrow - 1 + nrep - 1 + 2 * moves.astype(jnp.int32))

    is_source = row // here == rep
    first = (row - rep * here) * nrep
    own_chunk = row == rep * here + row // nrep

    def scatter(q):
        return remote(
            feat.at[pl.ds(q * share, share)], src.at[first + q], a1s.at[q], a1r.at[0], (first + q, rep)
        )

    for q in range(nrep):
        @pl.when(jnp.logical_and(is_source, first + q != row))
        def _():
            scatter(q).start()

        @pl.when(jnp.logical_and(is_source, first + q == row))
        def _():
            local = pltpu.make_async_copy(feat.at[pl.ds(q * share, share)], src.at[row], loc_sem)
            local.start()
            local.wait()

    my_feat = feat[pl.ds(pl.multiple_of(rep * share, share), share), :]
    base[...] = jnp.dot(my_feat, wself[...], preferred_element_type=F32)

    @pl.when(jnp.logical_not(own_chunk))
    def _():
        remote(src.at[row], src.at[row], a1s.at[0], a1r.at[0], partner).wait_recv()

    def gather(d):
        to = ((hi + d) % half) * PAIR + lo
        return remote(src.at[row], src.at[row], a2s.at[d - 1], a2r.at[d - 1], (to, rep))

    def share_pair(d):
        chunk = ((hi + half - d) % half) * PAIR + lo
        return remote(src.at[chunk], src.at[chunk], a3s.at[d], a3r.at[d], partner)

    for d in range(1, half):
        gather(d).start()
    share_pair(0).start()
    for d in range(1, half):
        gather(d).wait_recv()
        share_pair(d).start()
    for d in range(half):
        share_pair(d).wait_recv()
    adj_copy.wait()

    def partial(q):
        total = jnp.zeros((share, width), F32)
        for j in range(here):
            a = adj[j, pl.ds(pl.multiple_of(q * share, share), share), :]
            f = src[pl.ds(j * nrep, nrep)].reshape(rows, width)
            total = total + jnp.dot(a, f, preferred_element_type=F32)
        return total

    def send_part(d):
        to = (rep + d) % nrep
        return remote(part.at[d - 1], part_in.at[d - 1], bs.at[d - 1], br.at[d - 1], (row, to))

    for d in range(1, nrep):
        part[d - 1] = partial((rep + d) % nrep).astype(BF16)
        send_part(d).start()
    total = partial(rep)
    for d in range(1, nrep):
        send_part(d).wait_recv()
        total = total + part_in[d - 1].astype(F32)

    degree = deg[...]
    agg = (total / degree).astype(BF16)
    pre = base[...] + jnp.dot(agg, wneigh[...], preferred_element_type=F32)
    sig = jax.nn.sigmoid(pre)
    gpre = (cot[...].astype(F32) * sig * (1.0 + pre * (1.0 - sig))).astype(BF16)
    back_t = lax.dot_general(gpre, wneigh[...], (((1,), (1,)), ((), ())), preferred_element_type=F32)
    dagg[rep] = (back_t / degree).astype(BF16)

    def send_dagg(d):
        return remote(
            dagg.at[rep], dagg.at[rep], cs.at[d - 1], cr.at[d - 1], (row, (rep + d) % nrep)
        )

    for d in range(1, nrep):
        send_dagg(d).start()
    out[...] = (pre * sig).astype(BF16)
    ws = lax.dot_general(my_feat, gpre, (((0,), (0,)), ((), ())), preferred_element_type=F32)
    wn = lax.dot_general(agg, gpre, (((0,), (0,)), ((), ())), preferred_element_type=F32)
    piece = wpart.shape[1]
    wpart[pl.ds(0, half)] = ws.astype(BF16).reshape(half, piece, width)
    wpart[pl.ds(half, half)] = wn.astype(BF16).reshape(half, piece, width)

    def send_w1(d):
        to = (row + d) % nrow
        return remote(wpart.at[to], wrow_in.at[d - 1], w1s.at[d - 1], w1r.at[d - 1], (to, rep))

    for d in range(1, nrow):
        send_w1(d).start()
    base[...] = lax.dot_general(gpre, wself[...], (((1,), (1,)), ((), ())), preferred_element_type=F32)
    for d in range(1, nrep):
        remote(
            dagg.at[rep], dagg.at[(rep + nrep - d) % nrep], cs.at[d - 1], cr.at[d - 1], (row, rep)
        ).wait_recv()
    dagg_t[...] = dagg[...].reshape(rows, width).T

    unit = max(share, 128)
    per_unit = unit // share

    def send_pair(h):
        return remote(
            terms.at[h * PAIR + (1 - lo)], pair_in.at[h], d0s.at[h], d0r.at[h], partner
        )

    for u in range(here * rows // unit):
        j, col = divmod(u * unit, rows)
        t = jnp.dot(dagg_t[...], adj[j, :, col : col + unit], preferred_element_type=F32)
        terms[pl.ds(u * per_unit, per_unit)] = t.T.astype(BF16).reshape(per_unit, share, width)
        for r in range(u * per_unit, (u + 1) * per_unit):
            @pl.when(r % PAIR != lo)
            def _():
                send_pair(r // PAIR).start()

    wsum = wpart[row].astype(F32)
    for d in range(1, nrow):
        send_w1(d).wait_recv()
        wsum = wsum + wrow_in[d - 1].astype(F32)
    wrep_in[rep] = wsum.astype(BF16)

    def send_w2(d):
        return remote(
            wrep_in.at[rep], wrep_in.at[rep], w2s.at[d - 1], w2r.at[d - 1], (row, (rep + d) % nrep)
        )

    for d in range(1, nrep):
        send_w2(d).start()

    def send_plane(d):
        h = (hi + d) % half
        return remote(
            summed.at[h], plane_in.at[d - 1], d1s.at[d - 1], d1r.at[d - 1], (h * PAIR + lo, rep)
        )

    for d in list(range(1, half)) + [0]:
        h = (hi + d) % half
        send_pair(h).wait_recv()
        both = terms[h * PAIR + lo].astype(F32) + pair_in[h].astype(F32)
        if d > 0:
            summed[h] = both.astype(BF16)
            send_plane(d).start()

    for d in range(1, nrep):
        remote(
            wrep_in.at[rep], wrep_in.at[(rep + nrep - d) % nrep], w2s.at[d - 1], w2r.at[d - 1], (row, rep)
        ).wait_recv()
    wsum = wrep_in[0].astype(F32)
    for k in range(1, nrep):
        wsum = wsum + wrep_in[k].astype(F32)
    wall[row] = wsum.astype(BF16)

    def send_w3(d):
        return remote(
            wall.at[row], wall.at[row], w3s.at[d - 1], w3r.at[d - 1], ((row + d) % nrow, rep)
        )

    for d in range(1, nrow):
        send_w3(d).start()

    for d in range(1, half):
        send_plane(d).wait_recv()
        both = both + plane_in[d - 1].astype(F32)
    back[...] = both.astype(BF16)
    to_owner = remote(back, back_in, d2s, d2r, owner)

    @pl.when(moves)
    def _():
        to_owner.start()

    for d in range(1, nrow):
        remote(
            wall.at[row], wall.at[(row + nrow - d) % nrow], w3s.at[d - 1], w3r.at[d - 1], (row, rep)
        ).wait_recv()
    gself[...] = wall[pl.ds(0, half)].reshape(width, width).astype(F32)
    gneigh[...] = wall[pl.ds(half, half)].reshape(width, width).astype(F32)

    @pl.when(moves)
    def _():
        to_owner.wait_recv()
        gfeat[...] = (base[...] + back_in[...].astype(F32)).astype(BF16)

    @pl.when(jnp.logical_not(moves))
    def _():
        gfeat[...] = (base[...] + back[...].astype(F32)).astype(BF16)

    for q in range(nrep):
        @pl.when(jnp.logical_and(is_source, first + q != row))
        def _():
            scatter(q).wait_send()

    for d in range(1, half):
        gather(d).wait_send()
        send_plane(d).wait_send()
    for d in range(half):
        share_pair(d).wait_send()
        send_pair(d).wait_send()
    for d in range(1, nrep):
        send_part(d).wait_send()
        send_dagg(d).wait_send()
        send_w2(d).wait_send()
    for d in range(1, nrow):
        send_w1(d).wait_send()
        send_w3(d).wait_send()

    @pl.when(moves)
    def _():
        to_owner.wait_send()


def body(
    nrow, nrep,
    features, weight_self, weight_neigh, degrees, tile_values, tile_blocks, tile_count, cotangent,
):
    rows, width = features.shape
    here = tile_values.shape[1]
    share = rows // nrep
    half = nrow // PAIR
    piece = 2 * width // nrow
    adjacency = dense_adjacency(tile_values[0], tile_blocks[0], tile_count[0], rows)
    degree = lax.dynamic_slice_in_dim(degrees, lax.axis_index("rep") * share, share, 0)
    degree = degree.astype(F32)[:, None]
    sems = pltpu.SemaphoreType.DMA
    vmem = pl.BlockSpec(memory_space=pltpu.VMEM)
    return pl.pallas_call(
        functools.partial(layer_kernel, nrow, nrep, here),
        out_shape=(
            jax.ShapeDtypeStruct((share, width), BF16),
            jax.ShapeDtypeStruct((width, width), F32),
            jax.ShapeDtypeStruct((width, width), F32),
            jax.ShapeDtypeStruct((share, width), BF16),
        ),
        in_specs=[vmem] * 5 + [pl.BlockSpec(memory_space=pl.ANY)],
        out_specs=(vmem,) * 4,
        scratch_shapes=[
            pltpu.VMEM((here, rows, rows), BF16),
            pltpu.VMEM((nrow, share, width), BF16),
            pltpu.VMEM((nrep - 1, share, width), BF16),
            pltpu.VMEM((nrep - 1, share, width), BF16),
            pltpu.VMEM((nrep, share, width), BF16),
            pltpu.VMEM((width, rows), BF16),
            pltpu.VMEM((nrow, share, width), BF16),
            pltpu.VMEM((half, share, width), BF16),
            pltpu.VMEM((half, share, width), BF16),
            pltpu.VMEM((half - 1, share, width), BF16),
            pltpu.VMEM((share, width), BF16),
            pltpu.VMEM((share, width), BF16),
            pltpu.VMEM((nrow, piece, width), BF16),
            pltpu.VMEM((nrow - 1, piece, width), BF16),
            pltpu.VMEM((nrep, piece, width), BF16),
            pltpu.VMEM((nrow, piece, width), BF16),
            pltpu.VMEM((share, width), F32),
            sems, sems,
            sems((nrep,)), sems((1,)),
            sems((half - 1,)), sems((half - 1,)),
            sems((half,)), sems((half,)),
            sems((nrep - 1,)), sems((nrep - 1,)),
            sems((nrep - 1,)), sems((nrep - 1,)),
            sems((nrow - 1,)), sems((nrow - 1,)),
            sems((nrep - 1,)), sems((nrep - 1,)),
            sems((nrow - 1,)), sems((nrow - 1,)),
            sems((half,)), sems((half,)),
            sems((half - 1,)), sems((half - 1,)),
            sems, sems,
        ],
        compiler_params=pltpu.CompilerParams(collective_id=0, has_side_effects=True),
        name="layer",
    )(features, weight_self, weight_neigh, degree, cotangent, adjacency)


def solution(mesh):
    in_specs = (
        P("row", None),
        P(),
        P(),
        P("row"),
        P("row", "rep", None, None, None),
        P("row", "rep", None, None),
        P("row", "rep"),
        P(("row", "rep"), None),
    )
    out_specs = (P(("row", "rep"), None), P(), P(), P(("row", "rep"), None))
    run = functools.partial(body, mesh.shape["row"], mesh.shape["rep"])
    return jax.shard_map(run, mesh=mesh, in_specs=in_specs, out_specs=out_specs, check_vma=False)
```

time: 400 us -> 83.4 us (0.21)
  waiting for transfers between devices: 246 us -> 0 us
  Pallas kernels: 0 us -> 73.1 us
  blocking collectives: 72 us -> 0 us
  matrix products: 31.5 us -> 0 us
  local copies, waits for them, and re-layouts: 28 us -> 8.67 us
  between operations: 14 us -> 0.65 us
    psum x3 -> x0, waiting for transfers between devices: 218 us -> none  [the longest x1 132 us: body(): lax.psum((grad_self_part, grad_neigh_part), ('row', 'rep'))]
    pallas_call x0 -> x2, Pallas kernels: none -> 73.1 us  [the longest x1 69 us: body(): pl.pallas_call(functools.partial(layer_kernel, nrow, nrep, here), out_sha...]
    psum x1 -> x0, blocking collectives: 59.9 us -> none  [body(): summed = lax.psum(stacked, 'row')]
    dot_general x18 -> x0, matrix products: 31.5 us -> none  [the longest x2 6.46 us: body(): jnp.einsum('tij,tjf->tif', tile_values[0, section], picked, preferred_ele...]
    reduce_scatter x1 -> x0, waiting for transfers between devices: 27.3 us -> none  [body(): lax.psum_scatter(partial_value, 'rep', scatter_dimension=0, tiled=True)]
    dot_general x6 -> x0, local copies, waits for them, and re-layouts: 18.1 us -> none  [the longest x2 8.77 us: body(): jnp.einsum('tij,tjf->tif', tile_values[0, section], picked, preferred_ele...]
    all_gather x1 -> x0, blocking collectives: 12.2 us -> none  [body(): dagg_all = lax.all_gather(dagg_mine, 'rep', axis=0, tiled=True)]
  transfers between devices with their start and end apart: 4 -> 0, of which waited for: 4 -> 0; matrix products, arithmetic and copies ran while one was open for 3% -> 0% of each run, Pallas kernels for 0% -> 0%
where the time goes in v1:
time: 83.4 us; the launch traced here: 83.2 us
  Pallas kernels  73.1 us (88%)
  local copies, waits for them, and re-layouts  8.67 us (10%)
    pallas_call x1, Pallas kernels, body(): pl.pallas_call(functools.partial(layer_kernel, nrow, nrep, here), out_sha...  69 us
    unnamed x5, local copies, waits for them, and re-layouts  7.87 us
    pallas_call x1, Pallas kernels, dense_adjacency(): pl.pallas_call(dense_kernel, grid=(sections,), out_shape=jax.ShapeDtypeSt...  4.15 us

profile of v1, /device:TPU:7, one launch (start us, length us, event | category | flops | bytes accessed | tf_op | source)
XLA Modules:
  0.0 83.2 jit_solution(136229859689881392)
XLA Ops:
  0.6 0.8 dynamic-slice_convert_fusion
  1.4 1.4 %copy.13 = s32[1,2,48,2]{3,2,1,0:T(8,128)} copy(s32[1,2,48,2]{2,3,1,0:T(2,128)} %param.13) | data formatting | bytes 1536 | tf_op args[5]
  2.8 0.8 copy.14.deg
  3.6 4.2 %dense.1.adj_hbm = bf16[2,1024,1024]{2,1,0:T(8,128)(2,1)} custom-call(s32[2,48,2]{2,1,0:T(8,128)} %bitcast.5, s32[2]{0:T(128)} %bitcast.7, bf16[2,48,128,128]{3,2,1,0:T(8,128)(2,1)} %bitcast.4), custom_call_target="tpu_custom_call" | custom-call | tf_op jit(solution)/shard_map/dense/pallas_call | solution.py:33
  7.7 69.0 %layer.1 = (bf16[256,256]{1,0:T(8,128)(2,1)}, f32[256,256]{1,0:T(8,128)}, f32[256,256]{1,0:T(8,128)}, bf16[256,256]{1,0:T(8,128)(2,1)}) custom-call(bf16[1024,256]{1,0:T(8,128)(2,1)} %feat.1, bf16[256,256]{1,0:T(8,128)(2,1)} %wself.1, bf16[256,256]{1,0:T(8,128)(2,1)} %wneigh.1, f32[256,1]{1,0:T(8,128)} %copy.14.deg, bf16[256,256]{1,0:T(8,128)(2,1)} %cot.1, ...), custom_call_target="tpu_custom_call" | custom-call | tf_op jit(solution)/shard_map/layer/pallas_call | solution.py:319
  76.7 1.6 %copy.19 = bf16[256,256]{1,0:T(8,128)(2,1)} copy(bf16[256,256]{1,0:T(8,128)(2,1)} %get-tuple-element.8) | data formatting | bytes 262144
  78.3 1.7 %copy.20 = f32[256,256]{1,0:T(8,128)} copy(f32[256,256]{1,0:T(8,128)} %get-tuple-element.9) | data formatting | bytes 524288
  79.9 1.7 %copy.21 = f32[256,256]{1,0:T(8,128)} copy(f32[256,256]{1,0:T(8,128)} %get-tuple-element.10) | data formatting | bytes 524288
  81.6 1.6 %copy.22 = bf16[256,256]{1,0:T(8,128)(2,1)} copy(bf16[256,256]{1,0:T(8,128)(2,1)} %get-tuple-element.11) | data formatting | bytes 262144

commit v2 on v1

v2 whole, which is shorter than its diff:
```python
import functools

import jax
import jax.numpy as jnp
from jax import lax
from jax.experimental import pallas as pl
from jax.experimental.pallas import tpu as pltpu
from jax.sharding import PartitionSpec as P

MESH = pl.DeviceIdType.MESH
F32 = jnp.float32
BF16 = jnp.bfloat16
PAIR = 2


def dense_kernel(blocks_ref, count_ref, tiles_ref, out_ref, acc):
    section = pl.program_id(0)
    tile = tiles_ref.shape[-1]
    acc[...] = jnp.zeros_like(acc)

    def add(slot, carry):
        to = pl.multiple_of(blocks_ref[section, 0, slot] * tile, tile)
        src = pl.multiple_of(blocks_ref[section, 1, slot] * tile, tile)
        acc[pl.ds(to, tile), pl.ds(src, tile)] += tiles_ref[0, slot].astype(F32)
        return carry

    lax.fori_loop(0, count_ref[section], add, 0)
    out_ref[0] = acc[...].astype(BF16)


def dense_adjacency(tile_values, tile_blocks, tile_count, rows):
    sections, slots, tile, _ = tile_values.shape
    return pl.pallas_call(
        dense_kernel,
        grid=(sections,),
        out_shape=jax.ShapeDtypeStruct((sections, rows, rows), BF16),
        in_specs=[
            pl.BlockSpec(memory_space=pltpu.SMEM),
            pl.BlockSpec(memory_space=pltpu.SMEM),
            pl.BlockSpec((1, slots, tile, tile), lambda s: (s, 0, 0, 0)),
        ],
        out_specs=pl.BlockSpec((1, rows, rows), lambda s: (s, 0, 0)),
        scratch_shapes=[pltpu.VMEM((rows, rows), F32)],
        name="dense",
    )(tile_blocks, tile_count, tile_values)


def remote(src, dst, send, recv, device):
    return pltpu.make_async_remote_copy(
        src_ref=src, dst_ref=dst, send_sem=send, recv_sem=recv, device_id=device, device_id_type=MESH
    )


def layer_kernel(
    nrow, nrep, here,
    feat, wself, wneigh, deg, cot, adj_hbm,
    out, wall, gfeat,
    adj, own_feat, src, part, part_in, dagg, dagg_t, terms, pair_in, summed, plane_in, back, back_in,
    wpart, wrow_in, wrep_in, base, deg_col,
    adj_sem, loc_sem, a1s, a1r, a2s, a2r, a3s, a3r, bs, br, cs, cr, w1s, w1r, w2s, w2r, w3s, w3r,
    d0s, d0r, d1s, d1r, d2s, d2r,
):
    row, rep = lax.axis_index("row"), lax.axis_index("rep")
    rows, width = feat.shape
    lanes = src.shape[-1]
    slices = width // lanes
    share = rows // nrep
    half = nrow // PAIR
    hi, lo = row // PAIR, row % PAIR
    partner = (hi * PAIR + (1 - lo), rep)
    owner = (rep * here + row // nrep, row % nrep)
    giver = ((row % here) * nrep + rep, row // here)
    moves = jnp.logical_or(owner[0] != row, owner[1] != rep)

    adj_copy = pltpu.make_async_copy(adj_hbm, adj, adj_sem)
    adj_copy.start()

    barrier = pltpu.get_barrier_semaphore()

    def greet(device):
        pl.semaphore_signal(barrier, inc=1, device_id=device, device_id_type=MESH)

    for d in range(1, nrow):
        greet(((row + d) % nrow, rep))
    for d in range(1, nrep):
        greet((row, (rep + d) % nrep))

    @pl.when(moves)
    def _():
        greet(owner)
        greet(giver)

    for c in range(slices):
        own_feat[c] = feat[:, c * lanes : (c + 1) * lanes]

    pl.semaphore_wait(barrier, nrow - 1 + nrep - 1 + 2 * moves.astype(jnp.int32))

    is_source = row // here == rep
    first = (row - rep * here) * nrep
    own_chunk = row == rep * here + row // nrep

    def scatter(c, q):
        return remote(
            own_feat.at[c, pl.ds(q * share, share)], src.at[c, first + q],
            a1s.at[c, q], a1r.at[c], (first + q, rep),
        )

    for c in range(slices):
        for q in range(nrep):
            @pl.when(jnp.logical_and(is_source, first + q != row))
            def _():
                scatter(c, q).start()

            @pl.when(jnp.logical_and(is_source, first + q == row))
            def _():
                local = pltpu.make_async_copy(
                    own_feat.at[c, pl.ds(q * share, share)], src.at[c, row], loc_sem
                )
                local.start()
                local.wait()

    def gather(c, d):
        to = ((hi + d) % half) * PAIR + lo
        return remote(
            src.at[c, row], src.at[c, row], a2s.at[c, d - 1], a2r.at[c, d - 1], (to, rep)
        )

    def share_pair(c, d):
        chunk = ((hi + half - d) % half) * PAIR + lo
        return remote(src.at[c, chunk], src.at[c, chunk], a3s.at[c, d], a3r.at[c, d], partner)

    for c in range(slices):
        @pl.when(jnp.logical_not(own_chunk))
        def _():
            remote(src.at[c, row], src.at[c, row], a1s.at[c, 0], a1r.at[c], partner).wait_recv()

        for d in range(1, half):
            gather(c, d).start()
        share_pair(c, 0).start()

    my_feat = feat[pl.ds(pl.multiple_of(rep * share, share), share), :]
    base[...] = jnp.dot(my_feat, wself[...], preferred_element_type=F32)
    run = deg.shape[1]
    for b in range(rows // run):
        line = jnp.broadcast_to(deg[b : b + 1, :].astype(F32), (run, run))
        deg_col[pl.ds(b * run, run), :] = line.T
    adj_copy.wait()

    def partial(c, q):
        total = jnp.zeros((share, lanes), F32)
        for j in range(here):
            a = adj[j, pl.ds(pl.multiple_of(q * share, share), share), :]
            f = src[c, pl.ds(j * nrep, nrep)].reshape(rows, lanes)
            total = total + jnp.dot(a, f, preferred_element_type=F32)
        return total

    def send_part(c, d):
        to = (rep + d) % nrep
        return remote(
            part.at[c, d - 1], part_in.at[c, d - 1], bs.at[c, d - 1], br.at[c, d - 1], (row, to)
        )

    for c in range(slices):
        for d in range(1, half):
            gather(c, d).wait_recv()
            share_pair(c, d).start()
        for d in range(half):
            share_pair(c, d).wait_recv()
        for d in range(1, nrep):
            part[c, d - 1] = partial(c, (rep + d) % nrep).astype(BF16)
            send_part(c, d).start()
    degree = deg_col[pl.ds(pl.multiple_of(rep * share, share), share), :]
    aggs = []
    for c in range(slices):
        total = partial(c, rep)
        for d in range(1, nrep):
            send_part(c, d).wait_recv()
            total = total + part_in[c, d - 1].astype(F32)
        aggs.append((total / degree).astype(BF16))
    agg = jnp.concatenate(aggs, axis=1)

    pre = base[...] + jnp.dot(agg, wneigh[...], preferred_element_type=F32)
    sig = jax.nn.sigmoid(pre)
    gpre = (cot[...].astype(F32) * sig * (1.0 + pre * (1.0 - sig))).astype(BF16)

    def send_dagg(c, d):
        return remote(
            dagg.at[c, rep], dagg.at[c, rep], cs.at[c, d - 1], cr.at[c, d - 1],
            (row, (rep + d) % nrep),
        )

    for c in range(slices):
        back_t = lax.dot_general(
            gpre, wneigh[c * lanes : (c + 1) * lanes, :], (((1,), (1,)), ((), ())),
            preferred_element_type=F32,
        )
        dagg[c, rep] = (back_t / degree).astype(BF16)
        for d in range(1, nrep):
            send_dagg(c, d).start()
    ws = lax.dot_general(my_feat, gpre, (((0,), (0,)), ((), ())), preferred_element_type=F32)
    wn = lax.dot_general(agg, gpre, (((0,), (0,)), ((), ())), preferred_element_type=F32)
    piece = wpart.shape[1]
    wpart[pl.ds(0, half)] = ws.astype(BF16).reshape(half, piece, width)
    wpart[pl.ds(half, half)] = wn.astype(BF16).reshape(half, piece, width)

    def send_w1(d):
        to = (row + d) % nrow
        return remote(wpart.at[to], wrow_in.at[d - 1], w1s.at[d - 1], w1r.at[d - 1], (to, rep))

    for d in range(1, nrow):
        send_w1(d).start()
    out[...] = (pre * sig).astype(BF16)
    base[...] = lax.dot_general(gpre, wself[...], (((1,), (1,)), ((), ())), preferred_element_type=F32)

    unit = max(share, 128)
    per_unit = unit // share

    def send_pair(c, h):
        return remote(
            terms.at[c, h * PAIR + (1 - lo)], pair_in.at[c, h], d0s.at[c, h], d0r.at[c, h], partner
        )

    def send_plane(c, d):
        h = (hi + d) % half
        return remote(
            summed.at[c, h], plane_in.at[c, d - 1], d1s.at[c, d - 1], d1r.at[c, d - 1],
            (h * PAIR + lo, rep),
        )

    def to_owner(c):
        return remote(back.at[c], back_in.at[c], d2s.at[c], d2r.at[c], owner)

    def make_terms(c):
        for d in range(1, nrep):
            remote(
                dagg.at[c, rep], dagg.at[c, (rep + nrep - d) % nrep], cs.at[c, d - 1], cr.at[c, d - 1],
                (row, rep),
            ).wait_recv()
        dagg_t[...] = dagg[c].reshape(rows, lanes).T
        for u in range(here * rows // unit):
            j, col = divmod(u * unit, rows)
            t = jnp.dot(dagg_t[...], adj[j, :, col : col + unit], preferred_element_type=F32)
            terms[c, pl.ds(u * per_unit, per_unit)] = t.T.astype(BF16).reshape(per_unit, share, lanes)
            for r in range(u * per_unit, (u + 1) * per_unit):
                @pl.when(r % PAIR != lo)
                def _():
                    send_pair(c, r // PAIR).start()

    def add_pair(c):
        for d in list(range(1, half)) + [0]:
            h = (hi + d) % half
            send_pair(c, h).wait_recv()
            both = terms[c, h * PAIR + lo].astype(F32) + pair_in[c, h].astype(F32)
            if d > 0:
                summed[c, h] = both.astype(BF16)
                send_plane(c, d).start()
            else:
                back_sum[c] = both

    def add_plane(c):
        both = back_sum[c]
        for d in range(1, half):
            send_plane(c, d).wait_recv()
            both = both + plane_in[c, d - 1].astype(F32)
        back[c] = both.astype(BF16)

        @pl.when(moves)
        def _():
            to_owner(c).start()

    back_sum = {}
    for c in range(slices):
        make_terms(c)
        if c + 1 < slices:
            add_pair(c)

    wsum = wpart[row].astype(F32)
    for d in range(1, nrow):
        send_w1(d).wait_recv()
        wsum = wsum + wrow_in[d - 1].astype(F32)
    wrep_in[rep] = wsum.astype(BF16)

    def send_w2(d):
        return remote(
            wrep_in.at[rep], wrep_in.at[rep], w2s.at[d - 1], w2r.at[d - 1], (row, (rep + d) % nrep)
        )

    for d in range(1, nrep):
        send_w2(d).start()
    add_pair(slices - 1)
    for c in range(slices - 1):
        add_plane(c)

    for d in range(1, nrep):
        remote(
            wrep_in.at[rep], wrep_in.at[(rep + nrep - d) % nrep], w2s.at[d - 1], w2r.at[d - 1], (row, rep)
        ).wait_recv()
    wsum = wrep_in[0].astype(F32)
    for k in range(1, nrep):
        wsum = wsum + wrep_in[k].astype(F32)
    wall[row] = wsum.astype(BF16)

    def send_w3(d):
        return remote(
            wall.at[row], wall.at[row], w3s.at[d - 1], w3r.at[d - 1], ((row + d) % nrow, rep)
        )

    for d in range(1, nrow):
        send_w3(d).start()
    add_plane(slices - 1)
    for d in range(1, nrow):
        remote(
            wall.at[row], wall.at[(row + nrow - d) % nrow], w3s.at[d - 1], w3r.at[d - 1], (row, rep)
        ).wait_recv()

    for c in range(slices):
        cols = slice(c * lanes, (c + 1) * lanes)

        @pl.when(moves)
        def _():
            to_owner(c).wait_recv()
            gfeat[:, cols] = (base[:, cols] + back_in[c].astype(F32)).astype(BF16)

        @pl.when(jnp.logical_not(moves))
        def _():
            gfeat[:, cols] = (base[:, cols] + back[c].astype(F32)).astype(BF16)

    for c in range(slices):
        for q in range(nrep):
            @pl.when(jnp.logical_and(is_source, first + q != row))
            def _():
                scatter(c, q).wait_send()

        for d in range(1, half):
            gather(c, d).wait_send()
            send_plane(c, d).wait_send()
        for d in range(half):
            share_pair(c, d).wait_send()
            send_pair(c, d).wait_send()
        for d in range(1, nrep):
            send_part(c, d).wait_send()
            send_dagg(c, d).wait_send()

        @pl.when(moves)
        def _():
            to_owner(c).wait_send()

    for d in range(1, nrep):
        send_w2(d).wait_send()
    for d in range(1, nrow):
        send_w1(d).wait_send()
        send_w3(d).wait_send()


def close_kernel(out_in, wall, gfeat_in, out, gself, gneigh, gfeat):
    half = wall.shape[0] // 2
    out[...] = out_in[...]
    gfeat[...] = gfeat_in[...]
    gself[...] = wall[pl.ds(0, half)].reshape(gself.shape).astype(F32)
    gneigh[...] = wall[pl.ds(half, half)].reshape(gneigh.shape).astype(F32)


def body(
    nrow, nrep,
    features, weight_self, weight_neigh, degrees, tile_values, tile_blocks, tile_count, cotangent,
):
    rows, width = features.shape
    here = tile_values.shape[1]
    tile = tile_values.shape[-1]
    share = rows // nrep
    half = nrow // PAIR
    piece = 2 * width // nrow
    lanes = 128
    slices = width // lanes
    adjacency = dense_adjacency(
        tile_values[0], tile_blocks.transpose(0, 1, 3, 2)[0], tile_count[0], rows
    )
    sems = pltpu.SemaphoreType.DMA
    vmem = pl.BlockSpec(memory_space=pltpu.VMEM)

    def buf(*shape):
        return pltpu.VMEM(shape, BF16)

    out, wall, gfeat = pl.pallas_call(
        functools.partial(layer_kernel, nrow, nrep, here),
        out_shape=(
            jax.ShapeDtypeStruct((share, width), BF16),
            jax.ShapeDtypeStruct((nrow, piece, width), BF16),
            jax.ShapeDtypeStruct((share, width), BF16),
        ),
        in_specs=[vmem] * 5 + [pl.BlockSpec(memory_space=pl.ANY)],
        out_specs=(vmem,) * 3,
        scratch_shapes=[
            buf(here, rows, rows),
            buf(slices, rows, lanes),
            buf(slices, nrow, share, lanes),
            buf(slices, nrep - 1, share, lanes),
            buf(slices, nrep - 1, share, lanes),
            buf(slices, nrep, share, lanes),
            buf(lanes, rows),
            buf(slices, nrow, share, lanes),
            buf(slices, half, share, lanes),
            buf(slices, half, share, lanes),
            buf(slices, half - 1, share, lanes),
            buf(slices, share, lanes),
            buf(slices, share, lanes),
            buf(nrow, piece, width),
            buf(nrow - 1, piece, width),
            buf(nrep, piece, width),
            pltpu.VMEM((share, width), F32),
            pltpu.VMEM((rows, tile), F32),
            sems, sems,
            sems((slices, nrep)), sems((slices,)),
            sems((slices, half - 1)), sems((slices, half - 1)),
            sems((slices, half)), sems((slices, half)),
            sems((slices, nrep - 1)), sems((slices, nrep - 1)),
            sems((slices, nrep - 1)), sems((slices, nrep - 1)),
            sems((nrow - 1,)), sems((nrow - 1,)),
            sems((nrep - 1,)), sems((nrep - 1,)),
            sems((nrow - 1,)), sems((nrow - 1,)),
            sems((slices, half)), sems((slices, half)),
            sems((slices, half - 1)), sems((slices, half - 1)),
            sems((slices,)), sems((slices,)),
        ],
        compiler_params=pltpu.CompilerParams(collective_id=0, has_side_effects=True),
        name="layer",
    )(features, weight_self, weight_neigh, degrees.reshape(rows // tile, tile), cotangent, adjacency)
    out, grad_self, grad_neigh, gfeat = pl.pallas_call(
        close_kernel,
        out_shape=(
            jax.ShapeDtypeStruct((share, width), BF16),
            jax.ShapeDtypeStruct((width, width), F32),
            jax.ShapeDtypeStruct((width, width), F32),
            jax.ShapeDtypeStruct((share, width), BF16),
        ),
        in_specs=[vmem] * 3,
        out_specs=(vmem,) * 4,
        name="close",
    )(out, wall, gfeat)
    return out, grad_self, grad_neigh, gfeat


def solution(mesh):
    in_specs = (
        P("row", None),
        P(),
        P(),
        P("row"),
        P("row", "rep", None, None, None),
        P("row", "rep", None, None),
        P("row", "rep"),
        P(("row", "rep"), None),
    )
    out_specs = (P(("row", "rep"), None), P(), P(), P(("row", "rep"), None))
    run = functools.partial(body, mesh.shape["row"], mesh.shape["rep"])
    return jax.shard_map(run, mesh=mesh, in_specs=in_specs, out_specs=out_specs, check_vma=False)
```

time: 83.4 us -> 66.1 us (0.79)
  local copies, waits for them, and re-layouts: 8.67 us -> 0 us
  Pallas kernels: 73.1 us -> 65.1 us
    pallas_call x1, Pallas kernels: 69 us -> 58.9 us  [body(): pl.pallas_call(functools.partial(layer_kernel, nrow, nrep, here), out_sha...]
    unnamed x5 -> x0, local copies, waits for them, and re-layouts: 7.87 us -> none
    pallas_call x0 -> x1, Pallas kernels: none -> 1.95 us  [body(): pl.pallas_call(close_kernel, out_shape=(jax.ShapeDtypeStruct((share, widt...]
where the time goes in v2:
time: 66.1 us; the launch traced here: 65.8 us
  Pallas kernels  65.1 us (98%)
    pallas_call x1, Pallas kernels, body(): pl.pallas_call(functools.partial(layer_kernel, nrow, nrep, here), out_sha...  58.9 us
    pallas_call x1, Pallas kernels, dense_adjacency(): pl.pallas_call(dense_kernel, grid=(sections,), out_shape=jax.ShapeDtypeSt...  4.28 us
    pallas_call x1, Pallas kernels, body(): pl.pallas_call(close_kernel, out_shape=(jax.ShapeDtypeStruct((share, widt...  1.95 us

profile of v2, /device:TPU:7, one launch (start us, length us, event | category | flops | bytes accessed | tf_op | source)
XLA Modules:
  0.0 65.8 jit_solution(15050188754709693131)
XLA Ops:
  0.6 4.3 %dense.1.adj_hbm = bf16[2,1024,1024]{2,1,0:T(8,128)(2,1)} custom-call(s32[2,2,48]{2,1,0:T(2,128)} %bitcast.8, s32[2]{0:T(128)} %bitcast.9, bf16[2,48,128,128]{3,2,1,0:T(8,128)(2,1)} %bitcast.6), custom_call_target="tpu_custom_call" | custom-call | tf_op jit(solution)/shard_map/dense/pallas_call | solution.py:33
  4.9 58.9 %layer.1 = (bf16[256,256]{1,0:T(8,128)(2,1)}, bf16[8,64,256]{2,1,0:T(8,128)(2,1)}, bf16[256,256]{1,0:T(8,128)(2,1)}) custom-call(bf16[1024,256]{1,0:T(8,128)(2,1)} %feat.1, bf16[256,256]{1,0:T(8,128)(2,1)} %wself.1, bf16[256,256]{1,0:T(8,128)(2,1)} %wneigh.1, s32[8,128]{1,0:T(8,128)} %bitcast.7, bf16[256,256]{1,0:T(8,128)(2,1)} %cot.1, ...), custom_call_target="tpu_custom_call" | custom-call | tf_op jit(solution)/shard_map/layer/pallas_call | solution.py:384
  63.8 1.9 %close.1 = (bf16[256,256]{1,0:T(8,128)(2,1)}, f32[256,256]{1,0:T(8,128)}, f32[256,256]{1,0:T(8,128)}, bf16[256,256]{1,0:T(8,128)(2,1)}) custom-call(bf16[256,256]{1,0:T(8,128)(2,1)} %get-tuple-element.7.out_in, bf16[8,64,256]{2,1,0:T(8,128)(2,1)} %get-tuple-element.8.wall, bf16[256,256]{1,0:T(8,128)(2,1)} %get-tuple-element.9.gfeat_in), custom_call_target="tpu_custom_call" | custom-call | tf_op jit(solution)/shard_map/close/pallas_call | solution.py:428

commit v3 on v2

--- a/solution.py
+++ b/solution.py
@@ -57,7 +57,7 @@
     out, wall, gfeat,
     adj, own_feat, src, part, part_in, dagg, dagg_t, terms, pair_in, summed, plane_in, back, back_in,
     wpart, wrow_in, wrep_in, base, deg_col,
-    adj_sem, loc_sem, a1s, a1r, a2s, a2r, a3s, a3r, bs, br, cs, cr, w1s, w1r, w2s, w2r, w3s, w3r,
+    adj_sem, loc_sem, afs, a1s, a1r, a2s, a2r, a3s, a3r, bs, br, cs, fs, cr, w1s, w1r, w2s, w2r, w3s, w3r,
     d0s, d0r, d1s, d1r, d2s, d2r,
 ):
     row, rep = lax.axis_index("row"), lax.axis_index("rep")
@@ -90,14 +90,48 @@
         greet(owner)
         greet(giver)
 
+    def is_far(r, k):
+        return r // PAIR == half - 1 - (k * here) // PAIR
+
+    other = (rep + nrep - nrep // 2) % nrep
+    far_first = (row - other * here) * nrep
+    serves_far = row // here == other
+    far_me = is_far(row, rep)
+    far_source = (rep * here + row // nrep, (rep + nrep // 2) % nrep)
+
+    def sends_far(q):
+        return jnp.logical_and(serves_far, is_far(far_first + q, other))
+
+    expected = nrow - 1 + nrep - 1 + 2 * moves.astype(jnp.int32) + far_me.astype(jnp.int32)
+    for q in range(nrep):
+        expected = expected + sends_far(q).astype(jnp.int32)
+
+        @pl.when(sends_far(q))
+        def _():
+            greet((far_first + q, other))
+
+    @pl.when(far_me)
+    def _():
+        greet(far_source)
+
     for c in range(slices):
         own_feat[c] = feat[:, c * lanes : (c + 1) * lanes]
 
-    pl.semaphore_wait(barrier, nrow - 1 + nrep - 1 + 2 * moves.astype(jnp.int32))
+    pl.semaphore_wait(barrier, expected)
 
     is_source = row // here == rep
     first = (row - rep * here) * nrep
-    own_chunk = row == rep * here + row // nrep
+    own_chunk = jnp.logical_and(row == rep * here + row // nrep, jnp.logical_not(far_me))
+
+    def sends_near(q):
+        near = jnp.logical_and(is_source, jnp.logical_not(is_far(first + q, rep)))
+        return jnp.logical_and(near, first + q != row)
+
+    def scatter_far(c, q):
+        return remote(
+            own_feat.at[c, pl.ds(q * share, share)], src.at[c, far_first + q],
+            afs.at[c, q], a1r.at[c], (far_first + q, other),
+        )
 
     def scatter(c, q):
         return remote(
@@ -107,11 +141,15 @@
 
     for c in range(slices):
         for q in range(nrep):
-            @pl.when(jnp.logical_and(is_source, first + q != row))
+            @pl.when(sends_far(q))
+            def _():
+                scatter_far(c, q).start()
+
+            @pl.when(sends_near(q))
             def _():
                 scatter(c, q).start()
 
-            @pl.when(jnp.logical_and(is_source, first + q == row))
+            @pl.when(jnp.logical_and(own_chunk, first + q == row))
             def _():
                 local = pltpu.make_async_copy(
                     own_feat.at[c, pl.ds(q * share, share)], src.at[c, row], loc_sem
@@ -183,11 +221,25 @@
     sig = jax.nn.sigmoid(pre)
     gpre = (cot[...].astype(F32) * sig * (1.0 + pre * (1.0 - sig))).astype(BF16)
 
-    def send_dagg(c, d):
-        return remote(
-            dagg.at[c, rep], dagg.at[c, rep], cs.at[c, d - 1], cr.at[c, d - 1],
-            (row, (rep + d) % nrep),
-        )
+    direct = [(step, way) for step in (1, 2) if step < nrep for way in (1, -1)]
+
+    def within(k):
+        return jnp.logical_and(k >= 0, k < nrep)
+
+    def send_dagg(c, i):
+        step, way = direct[i]
+        return remote(
+            dagg.at[c, rep], dagg.at[c, rep], cs.at[c, i], cr.at[c, rep], (row, rep + way * step)
+        )
+
+    def pass_dagg(c, d, way):
+        origin = rep - way * d
+        return remote(
+            dagg.at[c, origin], dagg.at[c, origin], fs.at[c, origin], cr.at[c, origin], (row, rep + way)
+        )
+
+    def passes(d, way):
+        return jnp.logical_and(within(rep - way * d), within(rep + way))
 
     for c in range(slices):
         back_t = lax.dot_general(
@@ -195,8 +247,10 @@
             preferred_element_type=F32,
         )
         dagg[c, rep] = (back_t / degree).astype(BF16)
-        for d in range(1, nrep):
-            send_dagg(c, d).start()
+        for i in reversed(range(len(direct))):
+            @pl.when(within(rep + direct[i][1] * direct[i][0]))
+            def _():
+                send_dagg(c, i).start()
     ws = lax.dot_general(my_feat, gpre, (((0,), (0,)), ((), ())), preferred_element_type=F32)
     wn = lax.dot_general(agg, gpre, (((0,), (0,)), ((), ())), preferred_element_type=F32)
     piece = wpart.shape[1]
@@ -230,12 +284,21 @@
     def to_owner(c):
         return remote(back.at[c], back_in.at[c], d2s.at[c], d2r.at[c], owner)
 
+    def take_dagg(c, d):
+        for way in (1, -1):
+            @pl.when(within(rep - way * d))
+            def _():
+                origin = rep - way * d
+                remote(
+                    dagg.at[c, rep], dagg.at[c, origin], cs.at[c, 0], cr.at[c, origin], (row, rep)
+                ).wait_recv()
+
+            if d >= 2:
+                @pl.when(passes(d, way))
+                def _():
+                    pass_dagg(c, d, way).start()
+
     def make_terms(c):
-        for d in range(1, nrep):
-            remote(
-                dagg.at[c, rep], dagg.at[c, (rep + nrep - d) % nrep], cs.at[c, d - 1], cr.at[c, d - 1],
-                (row, rep),
-            ).wait_recv()
         dagg_t[...] = dagg[c].reshape(rows, lanes).T
         for u in range(here * rows // unit):
             j, col = divmod(u * unit, rows)
@@ -270,6 +333,8 @@
 
     back_sum = {}
     for c in range(slices):
+        for d in range(1, nrep):
+            take_dagg(c, d)
         make_terms(c)
         if c + 1 < slices:
             add_pair(c)
@@ -327,9 +392,13 @@
 
     for c in range(slices):
         for q in range(nrep):
-            @pl.when(jnp.logical_and(is_source, first + q != row))
+            @pl.when(sends_near(q))
             def _():
                 scatter(c, q).wait_send()
+
+            @pl.when(sends_far(q))
+            def _():
+                scatter_far(c, q).wait_send()
 
         for d in range(1, half):
             gather(c, d).wait_send()
@@ -339,7 +408,16 @@
             send_pair(c, d).wait_send()
         for d in range(1, nrep):
             send_part(c, d).wait_send()
-            send_dagg(c, d).wait_send()
+        for i in range(len(direct)):
+            @pl.when(within(rep + direct[i][1] * direct[i][0]))
+            def _():
+                send_dagg(c, i).wait_send()
+
+        for d in range(2, nrep):
+            for way in (1, -1):
+                @pl.when(passes(d, way))
+                def _():
+                    pass_dagg(c, d, way).wait_send()
 
         @pl.when(moves)
         def _():
@@ -410,11 +488,11 @@
             pltpu.VMEM((share, width), F32),
             pltpu.VMEM((rows, tile), F32),
             sems, sems,
-            sems((slices, nrep)), sems((slices,)),
+            sems((slices, nrep)), sems((slices, nrep)), sems((slices,)),
             sems((slices, half - 1)), sems((slices, half - 1)),
             sems((slices, half)), sems((slices, half)),
             sems((slices, nrep - 1)), sems((slices, nrep - 1)),
-            sems((slices, nrep - 1)), sems((slices, nrep - 1)),
+            sems((slices, 4)), sems((slices, nrep)), sems((slices, nrep)),
             sems((nrow - 1,)), sems((nrow - 1,)),
             sems((nrep - 1,)), sems((nrep - 1,)),
             sems((nrow - 1,)), sems((nrow - 1,)),

time: 66.1 us -> 67.5 us (1.021)
  Pallas kernels: 65.1 us -> 66.6 us
    pallas_call x1, Pallas kernels: 58.9 us -> 59.8 us  [body(): pl.pallas_call(functools.partial(layer_kernel, nrow, nrep, here), out_sha...]
where the time goes in v3:
time: 67.5 us; the launch traced here: 67.2 us
  Pallas kernels  66.6 us (99%)
    pallas_call x1, Pallas kernels, body(): pl.pallas_call(functools.partial(layer_kernel, nrow, nrep, here), out_sha...  59.8 us
    pallas_call x1, Pallas kernels, dense_adjacency(): pl.pallas_call(dense_kernel, grid=(sections,), out_shape=jax.ShapeDtypeSt...  4.81 us
    pallas_call x1, Pallas kernels, body(): pl.pallas_call(close_kernel, out_shape=(jax.ShapeDtypeStruct((share, widt...  1.95 us

profile of v3, /device:TPU:7, one launch (start us, length us, event | category | flops | bytes accessed | tf_op | source)
XLA Modules:
  0.0 67.2 jit_solution(8755923420014789761)
XLA Ops:
  0.6 4.8 %dense.1.adj_hbm = bf16[2,1024,1024]{2,1,0:T(8,128)(2,1)} custom-call(s32[2,2,48]{2,1,0:T(2,128)} %bitcast.8, s32[2]{0:T(128)} %bitcast.9, bf16[2,48,128,128]{3,2,1,0:T(8,128)(2,1)} %bitcast.6), custom_call_target="tpu_custom_call" | custom-call | tf_op jit(solution)/shard_map/dense/pallas_call | solution.py:33
  5.4 59.8 %layer.1 = (bf16[256,256]{1,0:T(8,128)(2,1)}, bf16[8,64,256]{2,1,0:T(8,128)(2,1)}, bf16[256,256]{1,0:T(8,128)(2,1)}) custom-call(bf16[1024,256]{1,0:T(8,128)(2,1)} %feat.1, bf16[256,256]{1,0:T(8,128)(2,1)} %wself.1, bf16[256,256]{1,0:T(8,128)(2,1)} %wneigh.1, s32[8,128]{1,0:T(8,128)} %bitcast.7, bf16[256,256]{1,0:T(8,128)(2,1)} %cot.1, ...), custom_call_target="tpu_custom_call" | custom-call | tf_op jit(solution)/shard_map/layer/pallas_call | solution.py:462
  65.2 1.9 %close.1 = (bf16[256,256]{1,0:T(8,128)(2,1)}, f32[256,256]{1,0:T(8,128)}, f32[256,256]{1,0:T(8,128)}, bf16[256,256]{1,0:T(8,128)(2,1)}) custom-call(bf16[256,256]{1,0:T(8,128)(2,1)} %get-tuple-element.7.out_in, bf16[8,64,256]{2,1,0:T(8,128)(2,1)} %get-tuple-element.8.wall, bf16[256,256]{1,0:T(8,128)(2,1)} %get-tuple-element.9.gfeat_in), custom_call_target="tpu_custom_call" | custom-call | tf_op jit(solution)/shard_map/close/pallas_call | solution.py:506

commit v4 on v2

--- a/solution.py
+++ b/solution.py
@@ -57,7 +57,7 @@
     out, wall, gfeat,
     adj, own_feat, src, part, part_in, dagg, dagg_t, terms, pair_in, summed, plane_in, back, back_in,
     wpart, wrow_in, wrep_in, base, deg_col,
-    adj_sem, loc_sem, a1s, a1r, a2s, a2r, a3s, a3r, bs, br, cs, cr, w1s, w1r, w2s, w2r, w3s, w3r,
+    adj_sem, loc_sem, afs, a1s, a1r, a2s, a2r, a3s, a3r, bs, br, cs, cr, w1s, w1r, w2s, w2r, w3s, w3r,
     d0s, d0r, d1s, d1r, d2s, d2r,
 ):
     row, rep = lax.axis_index("row"), lax.axis_index("rep")
@@ -90,14 +90,48 @@
         greet(owner)
         greet(giver)
 
+    def is_far(r, k):
+        return r // PAIR == half - 1 - (k * here) // PAIR
+
+    other = (rep + nrep - nrep // 2) % nrep
+    far_first = (row - other * here) * nrep
+    serves_far = row // here == other
+    far_me = is_far(row, rep)
+    far_source = (rep * here + row // nrep, (rep + nrep // 2) % nrep)
+
+    def sends_far(q):
+        return jnp.logical_and(serves_far, is_far(far_first + q, other))
+
+    expected = nrow - 1 + nrep - 1 + 2 * moves.astype(jnp.int32) + far_me.astype(jnp.int32)
+    for q in range(nrep):
+        expected = expected + sends_far(q).astype(jnp.int32)
+
+        @pl.when(sends_far(q))
+        def _():
+            greet((far_first + q, other))
+
+    @pl.when(far_me)
+    def _():
+        greet(far_source)
+
     for c in range(slices):
         own_feat[c] = feat[:, c * lanes : (c + 1) * lanes]
 
-    pl.semaphore_wait(barrier, nrow - 1 + nrep - 1 + 2 * moves.astype(jnp.int32))
+    pl.semaphore_wait(barrier, expected)
 
     is_source = row // here == rep
     first = (row - rep * here) * nrep
-    own_chunk = row == rep * here + row // nrep
+    own_chunk = jnp.logical_and(row == rep * here + row // nrep, jnp.logical_not(far_me))
+
+    def sends_near(q):
+        near = jnp.logical_and(is_source, jnp.logical_not(is_far(first + q, rep)))
+        return jnp.logical_and(near, first + q != row)
+
+    def scatter_far(c, q):
+        return remote(
+            own_feat.at[c, pl.ds(q * share, share)], src.at[c, far_first + q],
+            afs.at[c, q], a1r.at[c], (far_first + q, other),
+        )
 
     def scatter(c, q):
         return remote(
@@ -107,11 +141,15 @@
 
     for c in range(slices):
         for q in range(nrep):
-            @pl.when(jnp.logical_and(is_source, first + q != row))
+            @pl.when(sends_far(q))
+            def _():
+                scatter_far(c, q).start()
+
+            @pl.when(sends_near(q))
             def _():
                 scatter(c, q).start()
 
-            @pl.when(jnp.logical_and(is_source, first + q == row))
+            @pl.when(jnp.logical_and(own_chunk, first + q == row))
             def _():
                 local = pltpu.make_async_copy(
                     own_feat.at[c, pl.ds(q * share, share)], src.at[c, row], loc_sem
@@ -327,9 +365,13 @@
 
     for c in range(slices):
         for q in range(nrep):
-            @pl.when(jnp.logical_and(is_source, first + q != row))
+            @pl.when(sends_near(q))
             def _():
                 scatter(c, q).wait_send()
+
+            @pl.when(sends_far(q))
+            def _():
+                scatter_far(c, q).wait_send()
 
         for d in range(1, half):
             gather(c, d).wait_send()
@@ -410,7 +452,7 @@
             pltpu.VMEM((share, width), F32),
             pltpu.VMEM((rows, tile), F32),
             sems, sems,
-            sems((slices, nrep)), sems((slices,)),
+            sems((slices, nrep)), sems((slices, nrep)), sems((slices,)),
             sems((slices, half - 1)), sems((slices, half - 1)),
             sems((slices, half)), sems((slices, half)),
             sems((slices, nrep - 1)), sems((slices, nrep - 1)),

time: 66.1 us -> 67.9 us (1.027); the launches traced: 65.8 us -> 66.7 us
  Pallas kernels: 65.1 us -> 66 us
where the time goes in v4:
time: 67.9 us; the launch traced here: 66.7 us
  Pallas kernels  66 us (97%)
    pallas_call x1, Pallas kernels, body(): pl.pallas_call(functools.partial(layer_kernel, nrow, nrep, here), out_sha...  59.4 us
    pallas_call x1, Pallas kernels, dense_adjacency(): pl.pallas_call(dense_kernel, grid=(sections,), out_shape=jax.ShapeDtypeSt...  4.72 us
    pallas_call x1, Pallas kernels, body(): pl.pallas_call(close_kernel, out_shape=(jax.ShapeDtypeStruct((share, widt...  1.95 us

profile of v4, /device:TPU:7, one launch (start us, length us, event | category | flops | bytes accessed | tf_op | source)
XLA Modules:
  0.0 66.7 jit_solution(1937422995197409860)
XLA Ops:
  0.6 4.7 %dense.1.adj_hbm = bf16[2,1024,1024]{2,1,0:T(8,128)(2,1)} custom-call(s32[2,2,48]{2,1,0:T(2,128)} %bitcast.8, s32[2]{0:T(128)} %bitcast.9, bf16[2,48,128,128]{3,2,1,0:T(8,128)(2,1)} %bitcast.6), custom_call_target="tpu_custom_call" | custom-call | tf_op jit(solution)/shard_map/dense/pallas_call | solution.py:33
  5.3 59.4 %layer.1 = (bf16[256,256]{1,0:T(8,128)(2,1)}, bf16[8,64,256]{2,1,0:T(8,128)(2,1)}, bf16[256,256]{1,0:T(8,128)(2,1)}) custom-call(bf16[1024,256]{1,0:T(8,128)(2,1)} %feat.1, bf16[256,256]{1,0:T(8,128)(2,1)} %wself.1, bf16[256,256]{1,0:T(8,128)(2,1)} %wneigh.1, s32[8,128]{1,0:T(8,128)} %bitcast.7, bf16[256,256]{1,0:T(8,128)(2,1)} %cot.1, ...), custom_call_target="tpu_custom_call" | custom-call | tf_op jit(solution)/shard_map/layer/pallas_call | solution.py:426
  64.7 1.9 %close.1 = (bf16[256,256]{1,0:T(8,128)(2,1)}, f32[256,256]{1,0:T(8,128)}, f32[256,256]{1,0:T(8,128)}, bf16[256,256]{1,0:T(8,128)(2,1)}) custom-call(bf16[256,256]{1,0:T(8,128)(2,1)} %get-tuple-element.7.out_in, bf16[8,64,256]{2,1,0:T(8,128)(2,1)} %get-tuple-element.8.wall, bf16[256,256]{1,0:T(8,128)(2,1)} %get-tuple-element.9.gfeat_in), custom_call_target="tpu_custom_call" | custom-call | tf_op jit(solution)/shard_map/close/pallas_call | solution.py:470
